TPU v7x, 32 devices: a whole 2x2x4 slice. The times are simulated.
32 devices in a mesh: lon: 8 (over y, x, core), bal: 4 (over z).
Axes of the slice: x: 2, y: 2, z: 4, core: 2. Of those that a mesh axis runs over, the one named last changes fastest.
Arguments:
- conc: float32 [65536, 128], P(('lon', 'bal')), may hold values from -6 to 6
- neighbours: int32 [512, 8], P(('lon', 'bal')), may hold values from 0 to 511, as said below
- counts: int32 [512], P(('lon', 'bal')), may hold values from 1 to 8
- weights: int32 [512, 8], P(('lon', 'bal')), may hold values from 1 to 15
- zones: int32 [65536], P(('lon', 'bal')), may hold values from 0 to 31
- owners: int32 [65536, 1], P(('lon', 'bal')), may hold values from 0 to 3; in each aligned block of 2048 rows (0 to 2047, 2048 to 4095, ...) at most 1024 rows name the same one
- rate_table: float32 [32, 128], replicated, may hold values from 0.05 to 1
- reaction: bfloat16 [128, 128], replicated, may hold values from -0.5 to 0.5
Outputs:
- conc_out: bfloat16 [65536, 128], P(('lon', 'bal'))
- chem_slots: bfloat16 [131072, 128], P(('lon', 'bal'))
Inputs may be any that keep to these rules, and one draw needn't show every extreme that they name: neighbours[g, k] is a block of the same bal index as g, on the same longitude band or on the band just before or after it, with the bands wrapping around. On every trajectory owner, at most 1024 of its parcels have the same owners value; on some trajectory owners one value is taken exactly 1024 times.
All inputs are finite; a program needn't handle non-finite values.
Results may differ from a plain program's by a relative error of at most 0.0085.
Values may be sent and summed in bfloat16 or wider, within the bound.
No kernel may reach another device: no remote copies, remote signals or barrier semaphores. Data moves between devices by JAX's collectives and lax.ppermute only.
A program may use at most 64 MiB of HBM per device.

v0:
```python
import jax
import jax.numpy as jnp
from jax import lax
from jax.sharding import PartitionSpec as P

BLK = 128
KADJ = 8
ZONES = 32
SUBSTEPS = 12


def extended_2(cells, sides, width):
    for axis, dim in sides:
        count = lax.axis_size(axis)
        head = lax.slice_in_dim(cells, 0, width, axis=dim)
        tail = lax.slice_in_dim(cells, cells.shape[dim] - width, cells.shape[dim], axis=dim)
        cells = jnp.concatenate(
            [
                lax.ppermute(tail, axis, [(i, (i + 1) % count) for i in range(count)]),
                cells,
                lax.ppermute(head, axis, [((i + 1) % count, i) for i in range(count)]),
            ],
            axis=dim,
        )
    return cells


def shifted(value, axis, steps):
    count = lax.axis_size(axis)
    pairs = [(source, (source + steps) % count) for source in range(count)]
    return lax.ppermute(value, axis, pairs)


def chemistry(state, reaction):

    def advance(step_index, current):
        tendency = jnp.dot(
            current.astype(jnp.bfloat16), reaction, preferred_element_type=jnp.float32
        )
        return current + 0.25 * jnp.tanh(tendency)

    return lax.fori_loop(0, SUBSTEPS, advance, state.astype(jnp.float32)).astype(jnp.bfloat16)


def shards(conc, neighbours, counts, weights, zones, owners, rate_table, reaction):
    rows, width = conc.shape
    nblocks = rows // BLK
    lon_count = lax.axis_size("lon")
    bal_count = lax.axis_size("bal")
    device_count = lon_count * bal_count
    self_device = lax.axis_index("lon") * bal_count + lax.axis_index("bal")
    own_blocks = conc.reshape(nblocks, BLK, width)
    extended = extended_2(own_blocks, (("lon", 0),), nblocks)
    used = jnp.arange(KADJ, dtype=jnp.int32)[None, :] < counts[:, None]
    coefs = jnp.where(used, weights.astype(jnp.float32) / 128.0, 0.0)
    local_part = neighbours % nblocks
    apart = (neighbours // nblocks - self_device + device_count) % device_count
    ext_index = (
        jnp.where(apart == 0, nblocks, jnp.where(apart == bal_count, 2 * nblocks, 0)) + local_part
    )
    change = jnp.zeros((nblocks, BLK, width), jnp.float32)
    sent = jnp.zeros((3 * nblocks, BLK, width), jnp.float32)
    for column in range(KADJ):
        flux = coefs[:, column][:, None, None] * (extended[ext_index[:, column]] - own_blocks)
        change = change + flux
        sent = sent.at[ext_index[:, column]].add(flux)
    from_right = shifted(sent[:nblocks].astype(jnp.bfloat16), "lon", -1).astype(jnp.float32)
    from_left = shifted(sent[2 * nblocks :].astype(jnp.bfloat16), "lon", 1).astype(jnp.float32)
    change = change - sent[nblocks : 2 * nblocks] - from_right - from_left
    mixed = (own_blocks + change).reshape(rows, width)
    zone_table = (zones[:, None] == jnp.arange(ZONES, dtype=jnp.int32)[None, :]).astype(jnp.float32)
    rates = jnp.dot(zone_table, rate_table, precision=lax.Precision.HIGHEST)
    moved = (mixed * jnp.exp(-rates)).astype(jnp.bfloat16)
    capacity = 2 * rows // bal_count
    owner = owners[:, 0]
    owner_table = (owner[:, None] == jnp.arange(bal_count, dtype=jnp.int32)[None, :]).astype(
        jnp.int32
    )
    rank = jnp.sum((jnp.cumsum(owner_table, axis=0) - owner_table) * owner_table, axis=1)
    slot = owner * capacity + rank
    conc_out = chemistry(moved, reaction)
    outgoing = jnp.zeros((bal_count * capacity, width), jnp.bfloat16).at[slot].set(conc_out)
    outgoing = outgoing.reshape(bal_count, capacity, width)
    chem_slots = lax.all_to_all(outgoing, "bal", split_axis=0, concat_axis=0, tiled=True).reshape(
        -1, width
    )
    return (conc_out, chem_slots)


def solution(mesh):
    in_specs = (
        P(("lon", "bal"), None),
        P(("lon", "bal"), None),
        P(("lon", "bal")),
        P(("lon", "bal"), None),
        P(("lon", "bal")),
        P(("lon", "bal"), None),
        P(),
        P(),
    )
    out_specs = (P(("lon", "bal"), None), P(("lon", "bal"), None))
    return jax.shard_map(shards, mesh=mesh, in_specs=in_specs, out_specs=out_specs, check_vma=False)
```

profile of v0, /device:TPU:0, one launch (start us, length us, event | category | flops | bytes accessed | tf_op | source)
XLA Modules:
  0.0 134.0 jit_solution(15365341471317218973)
XLA Ops:
  1.2 2.9 %collective-permute-start.1 = (f32[16,128,128]{2,1,0:T(8,128)}, f32[16,128,128]{2,1,0:T(8,128)}, u32[]{:S(2)}, u32[]{:S(2)}) collective-permute-start(f32[16,128,128]{2,1,0:T(8,128)} %bitcast.69), channel_id=1, source_target_pairs={{4,0},{8,4},{12,8},{16,12},{20,16},{24,20},{28,24},{0,28},{5,1},{9... | collective-permute-start | bytes 3145736 | tf_op jit(solution)/shard_map/ppermute | solution.py:21
  7.9 17.5 %collective-permute-done = f32[16,128,128]{2,1,0:T(8,128)S(1)} collective-permute-done((f32[16,128,128]{2,1,0:T(8,128)}, f32[16,128,128]{2,1,0:T(8,128)S(1)}, u32[]{:S(2)}, u32[]{:S(2)}) %collective-permute-start) | collective-permute-done | bytes 1048608 | tf_op jit(solution)/shard_map/ppermute | solution.py:19
  27.0 2.1 %pad_maximum_fusion = f32[48,128,128]{2,1,0:T(8,128)S(1)} fusion(f32[16,128,128]{2,1,0:T(8,128)} %collective-permute-done.1, f32[16,128,128]{2,1,0:T(8,128)} %bitcast.70, f32[16,128,128]{2,1,0:T(8,128)} %copy-done.7), kind=kLoop, calls=%fused_computation.21 | loop fusion | flops 1572864 | bytes 6291456 | tf_op jit(solution)/shard_map/concatenate | solution.py:17
  29.0 1.6 %gather_fusion = f32[16,128,128]{2,1,0:T(8,128)} fusion(f32[48,128,128]{2,1,0:T(8,128)S(1)} %pad_maximum_fusion, s32[1024]{0:T(1024)S(1)} %get-tuple-element.59), kind=kCustom, calls=%fused_computation | custom fusion | bytes 2097216 | tf_op jit(solution)/shard_map/gather | solution.py:64
  30.6 1.6 %gather_fusion.1 = f32[16,128,128]{2,1,0:T(8,128)} fusion(f32[48,128,128]{2,1,0:T(8,128)S(1)} %pad_maximum_fusion, s32[1024]{0:T(1024)S(1)} %get-tuple-element.58), kind=kCustom, calls=%fused_computation.1 | custom fusion | bytes 2097216 | tf_op jit(solution)/shard_map/gather | solution.py:64
  32.3 1.6 %gather_fusion.2 = f32[16,128,128]{2,1,0:T(8,128)} fusion(f32[48,128,128]{2,1,0:T(8,128)S(1)} %pad_maximum_fusion, s32[1024]{0:T(1024)S(1)} %get-tuple-element.57), kind=kCustom, calls=%fused_computation.2 | custom fusion | bytes 2097216 | tf_op jit(solution)/shard_map/gather | solution.py:64
  37.1 1.6 %gather_fusion.5 = f32[16,128,128]{2,1,0:T(8,128)} fusion(f32[48,128,128]{2,1,0:T(8,128)S(1)} %pad_maximum_fusion, s32[1024]{0:T(1024)S(1)} %get-tuple-element.54), kind=kCustom, calls=%fused_computation.5 | custom fusion | bytes 2097216 | tf_op jit(solution)/shard_map/gather | solution.py:64
  38.7 1.6 %gather_fusion.6 = f32[16,128,128]{2,1,0:T(8,128)} fusion(f32[48,128,128]{2,1,0:T(8,128)S(1)} %pad_maximum_fusion, s32[1024]{0:T(1024)S(1)} %get-tuple-element.53), kind=kCustom, calls=%fused_computation.6 | custom fusion | bytes 2097216 | tf_op jit(solution)/shard_map/gather | solution.py:64
  41.9 7.7 %subtract_multiply_fusion = (f32[16,128,128]{2,1,0:T(8,128)}, f32[16,128,128]{2,1,0:T(8,128)}, f32[16,128,128]{2,1,0:T(8,128)}, f32[16,128,128]{2,1,0:T(8,128)},...) fusion(f32[16,128,128]{2,1,0:T(8,128)} %gather_fusion.7, ...), kind=kLoop, calls=%fused_computation.31 | loop fusion | flops 4194304 | bytes 17826304 | tf_op jit(solution)/shard_map/mul | solution.py:64
  50.0 2.6 %scatter_fusion = f32[48,128,128]{2,1,0:T(8,128)S(1)} fusion(f32[48,128,128]{2,1,0:T(8,128)S(1)} %broadcast_in_dim.15, s32[16]{0:T(128)S(1)} %get-tuple-element.51, f32[16,128,128]{2,1,0:T(8,128)} %get-tuple-element.35), kind=kCustom, calls=%fused_computation.8 | custom fusion | flops 262144 | bytes 3145792 | tf_op jit(solution)/shard_map/scatter-add | solution.py:66
  52.6 2.6 %scatter_fusion.1 = f32[48,128,128]{2,1,0:T(8,128)S(1)} fusion(f32[48,128,128]{2,1,0:T(8,128)S(1)} %scatter_fusion, s32[16]{0:T(128)S(1)} %get-tuple-element.50, f32[16,128,128]{2,1,0:T(8,128)} %get-tuple-element.34), kind=kCustom, calls=%fused_computation.9 | custom fusion | flops 262144 | bytes 3145792 | tf_op jit(solution)/shard_map/scatter-add | solution.py:66
  55.2 2.6 %scatter_fusion.2 = f32[48,128,128]{2,1,0:T(8,128)S(1)} fusion(f32[48,128,128]{2,1,0:T(8,128)S(1)} %scatter_fusion.1, s32[16]{0:T(128)S(1)} %get-tuple-element.49, f32[16,128,128]{2,1,0:T(8,128)} %get-tuple-element.33), kind=kCustom, calls=%fused_computation.10 | custom fusion | flops 262144 | bytes 3145792 | tf_op jit(solution)/shard_map/scatter-add | solution.py:66
  57.8 2.6 %scatter_fusion.3 = f32[48,128,128]{2,1,0:T(8,128)S(1)} fusion(f32[48,128,128]{2,1,0:T(8,128)S(1)} %scatter_fusion.2, s32[16]{0:T(128)S(1)} %get-tuple-element.48, f32[16,128,128]{2,1,0:T(8,128)} %get-tuple-element.32), kind=kCustom, calls=%fused_computation.11 | custom fusion | flops 262144 | bytes 3145792 | tf_op jit(solution)/shard_map/scatter-add | solution.py:66
  60.5 2.6 %scatter_fusion.4 = f32[48,128,128]{2,1,0:T(8,128)S(1)} fusion(f32[48,128,128]{2,1,0:T(8,128)S(1)} %scatter_fusion.3, s32[16]{0:T(128)S(1)} %get-tuple-element.47, f32[16,128,128]{2,1,0:T(8,128)} %get-tuple-element.31), kind=kCustom, calls=%fused_computation.12 | custom fusion | flops 262144 | bytes 3145792 | tf_op jit(solution)/shard_map/scatter-add | solution.py:66
  63.1 2.6 %scatter_fusion.5 = f32[48,128,128]{2,1,0:T(8,128)S(1)} fusion(f32[48,128,128]{2,1,0:T(8,128)S(1)} %scatter_fusion.4, s32[16]{0:T(128)S(1)} %get-tuple-element.46, f32[16,128,128]{2,1,0:T(8,128)} %get-tuple-element.30), kind=kCustom, calls=%fused_computation.13 | custom fusion | flops 262144 | bytes 3145792 | tf_op jit(solution)/shard_map/scatter-add | solution.py:66
  65.7 2.6 %scatter_fusion.6 = f32[48,128,128]{2,1,0:T(8,128)S(1)} fusion(f32[48,128,128]{2,1,0:T(8,128)S(1)} %scatter_fusion.5, s32[16]{0:T(128)S(1)} %get-tuple-element.45, f32[16,128,128]{2,1,0:T(8,128)} %get-tuple-element.29), kind=kCustom, calls=%fused_computation.14 | custom fusion | flops 262144 | bytes 3145792 | tf_op jit(solution)/shard_map/scatter-add | solution.py:66
  68.3 2.6 %scatter_fusion.7 = f32[48,128,128]{2,1,0:T(8,128)S(1)} fusion(f32[48,128,128]{2,1,0:T(8,128)S(1)} %scatter_fusion.6, s32[16]{0:T(128)S(1)} %get-tuple-element.44, f32[16,128,128]{2,1,0:T(8,128)} %get-tuple-element.28), kind=kCustom, calls=%fused_computation.15 | custom fusion | flops 262144 | bytes 3145792 | tf_op jit(solution)/shard_map/scatter-add | solution.py:66
  71.3 2.9 %collective-permute-start.2 = (bf16[16,128,128]{2,1,0:T(8,128)(2,1)S(1)}, bf16[16,128,128]{2,1,0:T(8,128)(2,1)S(1)}, u32[]{:S(2)}, u32[]{:S(2)}) collective-permute-start(bf16[16,128,128]{2,1,0:T(8,128)(2,1)S(1)} %get-tuple-element.26), channel_id=1, source_target_pairs={{0,28},{4,0},{8,4},{12,8},{16,12},{20,16},{24,20},{28,24},{1,29},{... | collective-permute-start | bytes 1572872 | tf_op jit(solution)/shard_map/ppermute | solution.py:31
  74.3 12.2 %collective-permute-done.2 = bf16[16,128,128]{2,1,0:T(8,128)(2,1)S(1)} collective-permute-done((bf16[16,128,128]{2,1,0:T(8,128)(2,1)S(1)}, bf16[16,128,128]{2,1,0:T(8,128)(2,1)S(1)}, u32[]{:S(2)}, u32[]{:S(2)}) %collective-permute-start.2) | collective-permute-done | bytes 524320 | tf_op jit(solution)/shard_map/ppermute | solution.py:31
  87.0 3.1 %fusion.6 = f32[16,128,128]{2,1,0:T(8,128)S(1)} fusion(f32[16,128,128]{2,1,0:T(8,128)} %bitcast.72, f32[48,128,128]{2,1,0:T(8,128)S(1)} %scatter_fusion.7, bf16[16,128,128]{2,1,0:T(8,128)(2,1)S(1)} %collective-permute-done.3, bf16[16,128,128]{2,1,0:T(8,128)(2,1)S(1)} %collective-permute-done.2, f32[16,128,128]{2,1,0:T(8,128)S(1)} %copy-done.1, ...), kind=kLoop, calls=%fused_computation.27 | loop fusion | flops 3407872 | bytes 12582912 | tf_op jit(solution)/shard_map/add | solution.py:70
  91.1 4.7 %while.10 = (s32[]{:T(128)}, f32[2048,128]{1,0:T(8,128)S(1)}, bf16[128,128]{1,0:T(8,128)(2,1)S(1)}, s32[]{:T(128)}) while((s32[]{:T(128)}, f32[2048,128]{1,0:T(8,128)S(1)}, bf16[128,128]{1,0:T(8,128)(2,1)S(1)}, s32[]{:T(128)}) %tuple.53), condition=%wide.region_9.10_spmd, body=%wide.region_8.9_spmd.sunk | while | flops 67895296 | bytes 4227125 | solution.py:42
  95.8 6.8 %scatter_custom_fusion.8 = bf16[4096,128]{1,0:T(8,128)(2,1)} fusion(s32[2048]{0:T(1024)S(1)} %bitcast.77, bf16[]{:T(256)} %constant.76.clone.1, f32[2048,128]{1,0:T(8,128)S(1)} %get-tuple-element.19), kind=kCustom, calls=%fused_computation.40 | custom fusion | flops 262144 | bytes 2097154 | tf_op jit(solution)/shard_map/scatter | solution.py:82
  102.6 5.6 %all-to-all-start = ((bf16[4,1024,128]{2,1,0:T(8,128)(2,1)}), bf16[4,1024,128]{2,1,0:T(8,128)(2,1)S(1)}, u32[]{:S(2)}, u32[]{:S(2)}) async-start(bf16[4,1024,128]{2,1,0:T(8,128)(2,1)} %bitcast.23), calls=%async_computation | async-start | bytes 2097152 | tf_op jit(solution)/shard_map/all_to_all | solution.py:84
  109.1 24.0 %all-to-all-done = bf16[4,1024,128]{2,1,0:T(8,128)(2,1)S(1)} async-done(((bf16[4,1024,128]{2,1,0:T(8,128)(2,1)}), bf16[4,1024,128]{2,1,0:T(8,128)(2,1)S(1)}, u32[]{:S(2)}, u32[]{:S(2)}) %all-to-all-start) | async-done | bytes 1048608 | tf_op jit(solution)/shard_map/all_to_all | solution.py:84
  (74 shorter events, 19.0 us)
Async XLA Ops:
  0.6 89.4 %copy-start = (f32[32,128]{1,0:T(8,128)S(1)}, f32[32,128]{1,0:T(8,128)}, u32[]{:S(2)}) copy-start(f32[32,128]{1,0:T(8,128)} %param.16) | copy-start | bytes 49156
  0.6 24.8 %collective-permute-start = (f32[16,128,128]{2,1,0:T(8,128)}, f32[16,128,128]{2,1,0:T(8,128)S(1)}, u32[]{:S(2)}, u32[]{:S(2)}) collective-permute-start(f32[16,128,128]{2,1,0:T(8,128)} %bitcast.68), channel_id=1, source_target_pairs={{0,4},{4,8},{8,12},{12,16},{16,20},{20,24},{24,28},{28,0},{1,5},{5... | collective-permute-start | bytes 3145736 | tf_op jit(solution)/shard_map/ppermute | solution.py:19
  1.2 25.8 %collective-permute-start.1 = (f32[16,128,128]{2,1,0:T(8,128)}, f32[16,128,128]{2,1,0:T(8,128)}, u32[]{:S(2)}, u32[]{:S(2)}) collective-permute-start(f32[16,128,128]{2,1,0:T(8,128)} %bitcast.69), channel_id=1, source_target_pairs={{4,0},{8,4},{12,8},{16,12},{20,16},{24,20},{28,24},{0,28},{5,1},{9... | collective-permute-start | bytes 3145736 | tf_op jit(solution)/shard_map/ppermute | solution.py:21
  25.4 1.0 copy-start.7
  70.9 3.3 %copy-start.9 = (s32[2048,1]{0,1:T(1,128)S(1)}, s32[2048,1]{0,1:T(1,128)}, u32[]{:S(2)}) copy-start(s32[2048,1]{0,1:T(1,128)} %param.15) | copy-start | bytes 24580
  70.9 16.0 %copy-start.1 = (f32[16,128,128]{2,1,0:T(8,128)S(1)}, f32[16,128,128]{2,1,0:T(8,128)}, u32[]{:S(2)}) copy-start(f32[16,128,128]{2,1,0:T(8,128)} %get-tuple-element.28) | copy-start | bytes 3145732
  70.9 16.0 %copy-start.2 = (f32[16,128,128]{2,1,0:T(8,128)S(1)}, f32[16,128,128]{2,1,0:T(8,128)}, u32[]{:S(2)}) copy-start(f32[16,128,128]{2,1,0:T(8,128)} %get-tuple-element.29) | copy-start | bytes 3145732
  71.0 16.0 %copy-start.3 = (f32[16,128,128]{2,1,0:T(8,128)S(1)}, f32[16,128,128]{2,1,0:T(8,128)}, u32[]{:S(2)}) copy-start(f32[16,128,128]{2,1,0:T(8,128)} %get-tuple-element.30) | copy-start | bytes 3145732
  71.0 16.0 %copy-start.4 = (f32[16,128,128]{2,1,0:T(8,128)S(1)}, f32[16,128,128]{2,1,0:T(8,128)}, u32[]{:S(2)}) copy-start(f32[16,128,128]{2,1,0:T(8,128)} %get-tuple-element.31) | copy-start | bytes 3145732
  71.0 16.0 %copy-start.5 = (f32[16,128,128]{2,1,0:T(8,128)S(1)}, f32[16,128,128]{2,1,0:T(8,128)}, u32[]{:S(2)}) copy-start(f32[16,128,128]{2,1,0:T(8,128)} %get-tuple-element.32) | copy-start | bytes 3145732
  71.0 16.0 %copy-start.6 = (f32[16,128,128]{2,1,0:T(8,128)S(1)}, f32[16,128,128]{2,1,0:T(8,128)}, u32[]{:S(2)}) copy-start(f32[16,128,128]{2,1,0:T(8,128)} %get-tuple-element.33) | copy-start | bytes 3145732
  71.3 15.2 %collective-permute-start.2 = (bf16[16,128,128]{2,1,0:T(8,128)(2,1)S(1)}, bf16[16,128,128]{2,1,0:T(8,128)(2,1)S(1)}, u32[]{:S(2)}, u32[]{:S(2)}) collective-permute-start(bf16[16,128,128]{2,1,0:T(8,128)(2,1)S(1)} %get-tuple-element.26), channel_id=1, source_target_pairs={{0,28},{4,0},{8,4},{12,8},{16,12},{20,16},{24,20},{28,24},{1,29},{... | collective-permute-start | bytes 1572872 | tf_op jit(solution)/shard_map/ppermute | solution.py:31
  74.2 12.7 %collective-permute-start.3 = (bf16[16,128,128]{2,1,0:T(8,128)(2,1)S(1)}, bf16[16,128,128]{2,1,0:T(8,128)(2,1)S(1)}, u32[]{:S(2)}, u32[]{:S(2)}) collective-permute-start(bf16[16,128,128]{2,1,0:T(8,128)(2,1)S(1)} %get-tuple-element.27), channel_id=1, source_target_pairs={{0,4},{4,8},{8,12},{12,16},{16,20},{20,24},{24,28},{28,0},{1,5},{5... | collective-permute-start | bytes 1572872 | tf_op jit(solution)/shard_map/ppermute | solution.py:31
  74.3 15.8 %copy-start.10 = (s32[2048]{0:T(1024)S(1)}, s32[2048]{0:T(1024)}, u32[]{:S(2)}) copy-start(s32[2048]{0:T(1024)} %param.14) | copy-start | bytes 24580
  74.3 16.8 %copy-start.8 = (bf16[128,128]{1,0:T(8,128)(2,1)S(1)}, bf16[128,128]{1,0:T(8,128)(2,1)}, u32[]{:S(2)}) copy-start(bf16[128,128]{1,0:T(8,128)(2,1)} %param.17) | copy-start | bytes 98308
  102.6 30.5 %all-to-all-start = ((bf16[4,1024,128]{2,1,0:T(8,128)(2,1)}), bf16[4,1024,128]{2,1,0:T(8,128)(2,1)S(1)}, u32[]{:S(2)}, u32[]{:S(2)}) async-start(bf16[4,1024,128]{2,1,0:T(8,128)(2,1)} %bitcast.23), calls=%async_computation | async-start | bytes 2097152 | tf_op jit(solution)/shard_map/all_to_all | solution.py:84
where the time goes:
time: 135 us; the launch traced here: 134 us
  waiting for transfers between devices  54.7 us (41%)
  other arithmetic  45.2 us (33%)
  local copies, waits for them, and re-layouts  16.3 us (12%)
  starting transfers between devices  12 us (9%)
  matrix products  4.52 us (3%)
    all_to_all x1, waiting for transfers between devices, shards(): lax.all_to_all(outgoing, 'bal', split_axis=0, concat_axis=0, tiled=True)  24 us
    scatter-add x8, other arithmetic, shards(): sent = sent.at[ext_index[:, column]].add(flux)  20.9 us
    ppermute x1, waiting for transfers between devices, extended_2(): lax.ppermute(tail, axis, [(i, (i + 1) % count) for i in range(count)])  17.5 us
    gather x8, local copies, waits for them, and re-layouts, shards(): extended[ext_index[:, column]] - own_blocks  12.9 us
    ppermute x2, waiting for transfers between devices, shifted(): return lax.ppermute(value, axis, pairs)  12.6 us
    mul x1, other arithmetic, shards(): coefs[:, column][:, None, None]  7.75 us
    scatter x1, other arithmetic, shards(): jnp.zeros((bal_count * capacity, width), jnp.bfloat16).at[slot]  6.78 us
    all_to_all x1, starting transfers between devices, shards(): lax.all_to_all(outgoing, 'bal', split_axis=0, concat_axis=0, tiled=True)  5.63 us
  transfers between devices with their start and end apart: 5, of which 5 were waited for; matrix products, arithmetic and copies ran while one was open for 3% of the time, Pallas kernels for 0%

commit v1 on v0

--- a/solution.py
+++ b/solution.py
@@ -1,3 +1,4 @@
+import functools
 import jax
 import jax.numpy as jnp
 from jax import lax
@@ -7,6 +8,34 @@
 KADJ = 8
 ZONES = 32
 SUBSTEPS = 12
+
+
+def note_stops_all_on_mesh(in_array, where_dim, sheet):
+    near, later = (in_array.shape[:where_dim], in_array.shape[where_dim + 1 :])
+    return jnp.moveaxis(in_array.reshape(*near, sheet, -1, *later), where_dim, 0)
+
+
+def _render_racks(field, ndim_at):
+    built = list(field.shape[1:])
+    built[ndim_at] *= field.shape[0]
+    return jnp.moveaxis(field, 0, ndim_at).reshape(built)
+
+
+def _turn_local_data(message, group_axis, raw, local_block):
+    a_now = lax.axis_size(group_axis)
+    y, u_next = (a_now, lax.axis_index(group_axis))
+    parts_out = note_stops_all_on_mesh(message, raw, y)
+    runs = [parts_out[u_next]]
+    for ii in range(1, y):
+        a_next = parts_out[u_next ^ ii]
+        runs.append(
+            lax.ppermute(a_next, axis_name=group_axis, perm=[(jj, jj ^ ii) for jj in range(y)])
+        )
+    parts_out = jnp.stack(runs, axis=0)[u_next ^ jnp.arange(y)]
+    return _render_racks(parts_out, local_block)
+
+
+begin_sheet = functools.partial(_turn_local_data, group_axis="bal", raw=0, local_block=0)
 
 
 def extended_2(cells, sides, width):
@@ -81,9 +110,7 @@
     conc_out = chemistry(moved, reaction)
     outgoing = jnp.zeros((bal_count * capacity, width), jnp.bfloat16).at[slot].set(conc_out)
     outgoing = outgoing.reshape(bal_count, capacity, width)
-    chem_slots = lax.all_to_all(outgoing, "bal", split_axis=0, concat_axis=0, tiled=True).reshape(
-        -1, width
-    )
+    chem_slots = begin_sheet(outgoing).reshape(-1, width)
     return (conc_out, chem_slots)
 
 

time: 135 us -> 130 us (0.963); the launches traced: 134 us -> 127 us
  waiting for transfers between devices: 54.7 us -> 48.6 us
    all_to_all x1 -> x0, waiting for transfers between devices: 24 us -> none  [shards(): lax.all_to_all(outgoing, 'bal', split_axis=0, concat_axis=0, tiled=True)]
    ppermute x0 -> x3, waiting for transfers between devices: none -> 17.9 us  [_turn_local_data(): lax.ppermute(a_next, axis_name=group_axis, perm=[(jj, jj ^ ii) for jj in...]
    all_to_all x1 -> x0, starting transfers between devices: 5.63 us -> none  [shards(): lax.all_to_all(outgoing, 'bal', split_axis=0, concat_axis=0, tiled=True)]
    ppermute x0 -> x3, starting transfers between devices: none -> 4.99 us  [_turn_local_data(): lax.ppermute(a_next, axis_name=group_axis, perm=[(jj, jj ^ ii) for jj in...]
    gather x0 -> x1, local copies, waits for them, and re-layouts: none -> 1.65 us  [_turn_local_data(): parts_out = jnp.stack(runs, axis=0)[u_next ^ jnp.arange(y)]]
  transfers between devices with their start and end apart: 5 -> 7, of which waited for: 5 -> 6; matrix products, arithmetic and copies ran while one was open for 3% -> 4% of each run, Pallas kernels for 0% -> 0%
where the time goes in v1:
time: 130 us; the launch traced here: 127 us
  waiting for transfers between devices  48.6 us (37%)
  other arithmetic  44.6 us (34%)
  local copies, waits for them, and re-layouts  17.1 us (13%)
  starting transfers between devices  11.3 us (9%)
  matrix products  4.52 us (3%)
    scatter-add x8, other arithmetic, shards(): sent = sent.at[ext_index[:, column]].add(flux)  20.9 us
    ppermute x3, waiting for transfers between devices, _turn_local_data(): lax.ppermute(a_next, axis_name=group_axis, perm=[(jj, jj ^ ii) for jj in...  17.9 us
    ppermute x1, waiting for transfers between devices, extended_2(): lax.ppermute(tail, axis, [(i, (i + 1) % count) for i in range(count)])  17.5 us
    gather x8, local copies, waits for them, and re-layouts, shards(): extended[ext_index[:, column]] - own_blocks  12.9 us
    ppermute x2, waiting for transfers between devices, shifted(): return lax.ppermute(value, axis, pairs)  12.6 us
    mul x1, other arithmetic, shards(): coefs[:, column][:, None, None]  7.75 us
    scatter x1, other arithmetic, shards(): jnp.zeros((bal_count * capacity, width), jnp.bfloat16).at[slot]  6.05 us
    ppermute x3, starting transfers between devices, _turn_local_data(): lax.ppermute(a_next, axis_name=group_axis, perm=[(jj, jj ^ ii) for jj in...  4.99 us
  transfers between devices with their start and end apart: 7, of which 6 were waited for; matrix products, arithmetic and copies ran while one was open for 4% of the time, Pallas kernels for 0%

profile of v1, /device:TPU:0, one launch (start us, length us, event | category | flops | bytes accessed | tf_op | source)
XLA Modules:
  0.0 127.5 jit_solution(8874972701164417663)
XLA Ops:
  1.2 2.9 %collective-permute-start.1 = (f32[16,128,128]{2,1,0:T(8,128)}, f32[16,128,128]{2,1,0:T(8,128)}, u32[]{:S(2)}, u32[]{:S(2)}) collective-permute-start(f32[16,128,128]{2,1,0:T(8,128)} %bitcast.82), channel_id=1, source_target_pairs={{4,0},{8,4},{12,8},{16,12},{20,16},{24,20},{28,24},{0,28},{5,1},{9... | collective-permute-start | bytes 3145736 | tf_op jit(solution)/shard_map/ppermute | solution.py:50
  7.9 17.5 %collective-permute-done = f32[16,128,128]{2,1,0:T(8,128)S(1)} collective-permute-done((f32[16,128,128]{2,1,0:T(8,128)}, f32[16,128,128]{2,1,0:T(8,128)S(1)}, u32[]{:S(2)}, u32[]{:S(2)}) %collective-permute-start) | collective-permute-done | bytes 1048608 | tf_op jit(solution)/shard_map/ppermute | solution.py:48
  27.0 2.1 %pad_maximum_fusion = f32[48,128,128]{2,1,0:T(8,128)S(1)} fusion(f32[16,128,128]{2,1,0:T(8,128)} %collective-permute-done.1, f32[16,128,128]{2,1,0:T(8,128)} %bitcast.83, f32[16,128,128]{2,1,0:T(8,128)} %copy-done.7), kind=kLoop, calls=%fused_computation.22 | loop fusion | flops 1572864 | bytes 6291456 | tf_op jit(solution)/shard_map/concatenate | solution.py:46
  30.6 1.6 %gather_fusion.1 = f32[16,128,128]{2,1,0:T(8,128)} fusion(f32[48,128,128]{2,1,0:T(8,128)S(1)} %pad_maximum_fusion, s32[1024]{0:T(1024)S(1)} %get-tuple-element.62), kind=kCustom, calls=%fused_computation.1 | custom fusion | bytes 2097216 | tf_op jit(solution)/shard_map/gather | solution.py:93
  37.1 1.6 %gather_fusion.5 = f32[16,128,128]{2,1,0:T(8,128)} fusion(f32[48,128,128]{2,1,0:T(8,128)S(1)} %pad_maximum_fusion, s32[1024]{0:T(1024)S(1)} %get-tuple-element.58), kind=kCustom, calls=%fused_computation.5 | custom fusion | bytes 2097216 | tf_op jit(solution)/shard_map/gather | solution.py:93
  41.9 7.7 %subtract_multiply_fusion = (f32[16,128,128]{2,1,0:T(8,128)}, f32[16,128,128]{2,1,0:T(8,128)}, f32[16,128,128]{2,1,0:T(8,128)}, f32[16,128,128]{2,1,0:T(8,128)},...) fusion(f32[16,128,128]{2,1,0:T(8,128)} %gather_fusion.7, ...), kind=kLoop, calls=%fused_computation.33 | loop fusion | flops 4194304 | bytes 17826304 | tf_op jit(solution)/shard_map/mul | solution.py:93
  50.0 2.6 %scatter_fusion = f32[48,128,128]{2,1,0:T(8,128)S(1)} fusion(f32[48,128,128]{2,1,0:T(8,128)S(1)} %broadcast_in_dim.15, s32[16]{0:T(128)S(1)} %get-tuple-element.55, f32[16,128,128]{2,1,0:T(8,128)} %get-tuple-element.39), kind=kCustom, calls=%fused_computation.9 | custom fusion | flops 262144 | bytes 3145792 | tf_op jit(solution)/shard_map/scatter-add | solution.py:95
  52.6 2.6 %scatter_fusion.1 = f32[48,128,128]{2,1,0:T(8,128)S(1)} fusion(f32[48,128,128]{2,1,0:T(8,128)S(1)} %scatter_fusion, s32[16]{0:T(128)S(1)} %get-tuple-element.54, f32[16,128,128]{2,1,0:T(8,128)} %get-tuple-element.38), kind=kCustom, calls=%fused_computation.10 | custom fusion | flops 262144 | bytes 3145792 | tf_op jit(solution)/shard_map/scatter-add | solution.py:95
  55.2 2.6 %scatter_fusion.2 = f32[48,128,128]{2,1,0:T(8,128)S(1)} fusion(f32[48,128,128]{2,1,0:T(8,128)S(1)} %scatter_fusion.1, s32[16]{0:T(128)S(1)} %get-tuple-element.53, f32[16,128,128]{2,1,0:T(8,128)} %get-tuple-element.37), kind=kCustom, calls=%fused_computation.11 | custom fusion | flops 262144 | bytes 3145792 | tf_op jit(solution)/shard_map/scatter-add | solution.py:95
  57.8 2.6 %scatter_fusion.3 = f32[48,128,128]{2,1,0:T(8,128)S(1)} fusion(f32[48,128,128]{2,1,0:T(8,128)S(1)} %scatter_fusion.2, s32[16]{0:T(128)S(1)} %get-tuple-element.52, f32[16,128,128]{2,1,0:T(8,128)} %get-tuple-element.36), kind=kCustom, calls=%fused_computation.12 | custom fusion | flops 262144 | bytes 3145792 | tf_op jit(solution)/shard_map/scatter-add | solution.py:95
  60.5 2.6 %scatter_fusion.4 = f32[48,128,128]{2,1,0:T(8,128)S(1)} fusion(f32[48,128,128]{2,1,0:T(8,128)S(1)} %scatter_fusion.3, s32[16]{0:T(128)S(1)} %get-tuple-element.51, f32[16,128,128]{2,1,0:T(8,128)} %get-tuple-element.35), kind=kCustom, calls=%fused_computation.13 | custom fusion | flops 262144 | bytes 3145792 | tf_op jit(solution)/shard_map/scatter-add | solution.py:95
  63.1 2.6 %scatter_fusion.5 = f32[48,128,128]{2,1,0:T(8,128)S(1)} fusion(f32[48,128,128]{2,1,0:T(8,128)S(1)} %scatter_fusion.4, s32[16]{0:T(128)S(1)} %get-tuple-element.50, f32[16,128,128]{2,1,0:T(8,128)} %get-tuple-element.34), kind=kCustom, calls=%fused_computation.14 | custom fusion | flops 262144 | bytes 3145792 | tf_op jit(solution)/shard_map/scatter-add | solution.py:95
  65.7 2.6 %scatter_fusion.6 = f32[48,128,128]{2,1,0:T(8,128)S(1)} fusion(f32[48,128,128]{2,1,0:T(8,128)S(1)} %scatter_fusion.5, s32[16]{0:T(128)S(1)} %get-tuple-element.49, f32[16,128,128]{2,1,0:T(8,128)} %get-tuple-element.33), kind=kCustom, calls=%fused_computation.15 | custom fusion | flops 262144 | bytes 3145792 | tf_op jit(solution)/shard_map/scatter-add | solution.py:95
  68.3 2.6 %scatter_fusion.7 = f32[48,128,128]{2,1,0:T(8,128)S(1)} fusion(f32[48,128,128]{2,1,0:T(8,128)S(1)} %scatter_fusion.6, s32[16]{0:T(128)S(1)} %get-tuple-element.48, f32[16,128,128]{2,1,0:T(8,128)} %get-tuple-element.32), kind=kCustom, calls=%fused_computation.16 | custom fusion | flops 262144 | bytes 3145792 | tf_op jit(solution)/shard_map/scatter-add | solution.py:95
  71.3 2.9 %collective-permute-start.2 = (bf16[16,128,128]{2,1,0:T(8,128)(2,1)S(1)}, bf16[16,128,128]{2,1,0:T(8,128)(2,1)S(1)}, u32[]{:S(2)}, u32[]{:S(2)}) collective-permute-start(bf16[16,128,128]{2,1,0:T(8,128)(2,1)S(1)} %get-tuple-element.26), channel_id=1, source_target_pairs={{0,28},{4,0},{8,4},{12,8},{16,12},{20,16},{24,20},{28,24},{1,29},{... | collective-permute-start | bytes 1572872 | tf_op jit(solution)/shard_map/ppermute | solution.py:60
  74.3 12.2 %collective-permute-done.2 = bf16[16,128,128]{2,1,0:T(8,128)(2,1)S(1)} collective-permute-done((bf16[16,128,128]{2,1,0:T(8,128)(2,1)S(1)}, bf16[16,128,128]{2,1,0:T(8,128)(2,1)S(1)}, u32[]{:S(2)}, u32[]{:S(2)}) %collective-permute-start.2) | collective-permute-done | bytes 524320 | tf_op jit(solution)/shard_map/ppermute | solution.py:60
  87.0 3.1 %fusion.6 = f32[16,128,128]{2,1,0:T(8,128)S(1)} fusion(f32[16,128,128]{2,1,0:T(8,128)} %bitcast.85, f32[48,128,128]{2,1,0:T(8,128)S(1)} %scatter_fusion.7, bf16[16,128,128]{2,1,0:T(8,128)(2,1)S(1)} %collective-permute-done.3, bf16[16,128,128]{2,1,0:T(8,128)(2,1)S(1)} %collective-permute-done.2, f32[16,128,128]{2,1,0:T(8,128)S(1)} %copy-done.1, ...), kind=kLoop, calls=%fused_computation.28 | loop fusion | flops 3407872 | bytes 12582912 | tf_op jit(solution)/shard_map/add | solution.py:99
  91.1 4.7 %while.10 = (s32[]{:T(128)}, f32[2048,128]{1,0:T(8,128)S(1)}, bf16[128,128]{1,0:T(8,128)(2,1)S(1)}, s32[]{:T(128)}) while((s32[]{:T(128)}, f32[2048,128]{1,0:T(8,128)S(1)}, bf16[128,128]{1,0:T(8,128)(2,1)S(1)}, s32[]{:T(128)}) %tuple.54), condition=%wide.region_9.10_spmd, body=%wide.region_8.9_spmd.sunk | while | flops 67895296 | bytes 4227125 | solution.py:71
  95.8 6.0 %scatter_custom_fusion.8 = bf16[4096,128]{1,0:T(8,128)(2,1)S(1)} fusion(s32[2048]{0:T(1024)S(1)} %bitcast.94, bf16[]{:T(256)} %constant.81.clone.1, f32[2048,128]{1,0:T(8,128)S(1)} %get-tuple-element.19), kind=kCustom, calls=%fused_computation.42 | custom fusion | flops 262144 | bytes 2097154 | tf_op jit(solution)/shard_map/scatter | solution.py:111
  102.0 2.4 %collective-permute-start.4 = (bf16[1,1024,128]{2,1,0:T(8,128)(2,1)S(1)}, bf16[1,1024,128]{2,1,0:T(8,128)(2,1)S(1)}, u32[]{:S(2)}, u32[]{:S(2)}) collective-permute-start(bf16[1,1024,128]{2,1,0:T(8,128)(2,1)S(1)} %get-tuple-element.31), channel_id=1, source_target_pairs={{0,1},{1,0},{2,3},{3,2},{4,5},{5,4},{6,7},{7,6},{8,9},{9,8},{10,11... | collective-permute-start | bytes 786440 | tf_op jit(solution)/shard_map/ppermute | solution.py:32
  104.4 2.6 %collective-permute-start.5 = (bf16[1,1024,128]{2,1,0:T(8,128)(2,1)S(1)}, bf16[1,1024,128]{2,1,0:T(8,128)(2,1)S(1)}, u32[]{:S(2)}, u32[]{:S(2)}) collective-permute-start(bf16[1,1024,128]{2,1,0:T(8,128)(2,1)S(1)} %get-tuple-element.30), channel_id=1, source_target_pairs={{0,2},{1,3},{2,0},{3,1},{4,6},{5,7},{6,4},{7,5},{8,10},{9,11},{10,... | collective-permute-start | bytes 786440 | tf_op jit(solution)/shard_map/ppermute | solution.py:32
  107.8 6.6 %collective-permute-done.4 = bf16[1,1024,128]{2,1,0:T(8,128)(2,1)S(1)} collective-permute-done((bf16[1,1024,128]{2,1,0:T(8,128)(2,1)S(1)}, bf16[1,1024,128]{2,1,0:T(8,128)(2,1)S(1)}, u32[]{:S(2)}, u32[]{:S(2)}) %collective-permute-start.4) | collective-permute-done | bytes 262176 | tf_op jit(solution)/shard_map/ppermute | solution.py:32
  114.4 11.3 %collective-permute-done.5 = bf16[1,1024,128]{2,1,0:T(8,128)(2,1)S(1)} collective-permute-done((bf16[1,1024,128]{2,1,0:T(8,128)(2,1)S(1)}, bf16[1,1024,128]{2,1,0:T(8,128)(2,1)S(1)}, u32[]{:S(2)}, u32[]{:S(2)}) %collective-permute-start.5) | collective-permute-done | bytes 262176 | tf_op jit(solution)/shard_map/ppermute | solution.py:32
  125.8 1.7 %gather_fusion.8 = bf16[4,1024,128]{2,1,0:T(8,128)(2,1)} fusion(bf16[4,1024,128]{2,1,0:T(8,128)(2,1)S(1)} %maximum_bitcast_fusion, s32[1024]{0:T(1024)S(1)} %pad_clamp_fusion), kind=kCustom, calls=%fused_computation.8 | custom fusion | bytes 2097168 | tf_op jit(solution)/shard_map/gather | solution.py:34
  (82 shorter events, 23.1 us)
Async XLA Ops:
  0.6 89.4 %copy-start = (f32[32,128]{1,0:T(8,128)S(1)}, f32[32,128]{1,0:T(8,128)}, u32[]{:S(2)}) copy-start(f32[32,128]{1,0:T(8,128)} %param.16) | copy-start | bytes 49156
  0.6 24.8 %collective-permute-start = (f32[16,128,128]{2,1,0:T(8,128)}, f32[16,128,128]{2,1,0:T(8,128)S(1)}, u32[]{:S(2)}, u32[]{:S(2)}) collective-permute-start(f32[16,128,128]{2,1,0:T(8,128)} %bitcast.81), channel_id=1, source_target_pairs={{0,4},{4,8},{8,12},{12,16},{16,20},{20,24},{24,28},{28,0},{1,5},{5... | collective-permute-start | bytes 3145736 | tf_op jit(solution)/shard_map/ppermute | solution.py:48
  1.2 25.8 %collective-permute-start.1 = (f32[16,128,128]{2,1,0:T(8,128)}, f32[16,128,128]{2,1,0:T(8,128)}, u32[]{:S(2)}, u32[]{:S(2)}) collective-permute-start(f32[16,128,128]{2,1,0:T(8,128)} %bitcast.82), channel_id=1, source_target_pairs={{4,0},{8,4},{12,8},{16,12},{20,16},{24,20},{28,24},{0,28},{5,1},{9... | collective-permute-start | bytes 3145736 | tf_op jit(solution)/shard_map/ppermute | solution.py:50
  25.4 1.0 copy-start.7
  70.9 3.3 %copy-start.9 = (s32[2048,1]{0,1:T(1,128)S(1)}, s32[2048,1]{0,1:T(1,128)}, u32[]{:S(2)}) copy-start(s32[2048,1]{0,1:T(1,128)} %param.15) | copy-start | bytes 24580
  70.9 16.0 %copy-start.1 = (f32[16,128,128]{2,1,0:T(8,128)S(1)}, f32[16,128,128]{2,1,0:T(8,128)}, u32[]{:S(2)}) copy-start(f32[16,128,128]{2,1,0:T(8,128)} %get-tuple-element.32) | copy-start | bytes 3145732
  70.9 16.0 %copy-start.2 = (f32[16,128,128]{2,1,0:T(8,128)S(1)}, f32[16,128,128]{2,1,0:T(8,128)}, u32[]{:S(2)}) copy-start(f32[16,128,128]{2,1,0:T(8,128)} %get-tuple-element.33) | copy-start | bytes 3145732
  71.0 16.0 %copy-start.3 = (f32[16,128,128]{2,1,0:T(8,128)S(1)}, f32[16,128,128]{2,1,0:T(8,128)}, u32[]{:S(2)}) copy-start(f32[16,128,128]{2,1,0:T(8,128)} %get-tuple-element.34) | copy-start | bytes 3145732
  71.0 16.0 %copy-start.4 = (f32[16,128,128]{2,1,0:T(8,128)S(1)}, f32[16,128,128]{2,1,0:T(8,128)}, u32[]{:S(2)}) copy-start(f32[16,128,128]{2,1,0:T(8,128)} %get-tuple-element.35) | copy-start | bytes 3145732
  71.0 16.0 %copy-start.5 = (f32[16,128,128]{2,1,0:T(8,128)S(1)}, f32[16,128,128]{2,1,0:T(8,128)}, u32[]{:S(2)}) copy-start(f32[16,128,128]{2,1,0:T(8,128)} %get-tuple-element.36) | copy-start | bytes 3145732
  71.0 16.0 %copy-start.6 = (f32[16,128,128]{2,1,0:T(8,128)S(1)}, f32[16,128,128]{2,1,0:T(8,128)}, u32[]{:S(2)}) copy-start(f32[16,128,128]{2,1,0:T(8,128)} %get-tuple-element.37) | copy-start | bytes 3145732
  71.3 15.2 %collective-permute-start.2 = (bf16[16,128,128]{2,1,0:T(8,128)(2,1)S(1)}, bf16[16,128,128]{2,1,0:T(8,128)(2,1)S(1)}, u32[]{:S(2)}, u32[]{:S(2)}) collective-permute-start(bf16[16,128,128]{2,1,0:T(8,128)(2,1)S(1)} %get-tuple-element.26), channel_id=1, source_target_pairs={{0,28},{4,0},{8,4},{12,8},{16,12},{20,16},{24,20},{28,24},{1,29},{... | collective-permute-start | bytes 1572872 | tf_op jit(solution)/shard_map/ppermute | solution.py:60
  74.2 12.7 %collective-permute-start.3 = (bf16[16,128,128]{2,1,0:T(8,128)(2,1)S(1)}, bf16[16,128,128]{2,1,0:T(8,128)(2,1)S(1)}, u32[]{:S(2)}, u32[]{:S(2)}) collective-permute-start(bf16[16,128,128]{2,1,0:T(8,128)(2,1)S(1)} %get-tuple-element.27), channel_id=1, source_target_pairs={{0,4},{4,8},{8,12},{12,16},{16,20},{20,24},{24,28},{28,0},{1,5},{5... | collective-permute-start | bytes 1572872 | tf_op jit(solution)/shard_map/ppermute | solution.py:60
  74.3 15.8 %copy-start.10 = (s32[2048]{0:T(1024)S(1)}, s32[2048]{0:T(1024)}, u32[]{:S(2)}) copy-start(s32[2048]{0:T(1024)} %param.14) | copy-start | bytes 24580
  74.3 16.8 %copy-start.8 = (bf16[128,128]{1,0:T(8,128)(2,1)S(1)}, bf16[128,128]{1,0:T(8,128)(2,1)}, u32[]{:S(2)}) copy-start(bf16[128,128]{1,0:T(8,128)(2,1)} %param.17) | copy-start | bytes 98308
  102.0 12.4 %collective-permute-start.4 = (bf16[1,1024,128]{2,1,0:T(8,128)(2,1)S(1)}, bf16[1,1024,128]{2,1,0:T(8,128)(2,1)S(1)}, u32[]{:S(2)}, u32[]{:S(2)}) collective-permute-start(bf16[1,1024,128]{2,1,0:T(8,128)(2,1)S(1)} %get-tuple-element.31), channel_id=1, source_target_pairs={{0,1},{1,0},{2,3},{3,2},{4,5},{5,4},{6,7},{7,6},{8,9},{9,8},{10,11... | collective-permute-start | bytes 786440 | tf_op jit(solution)/shard_map/ppermute | solution.py:32
  104.4 21.3 %collective-permute-start.5 = (bf16[1,1024,128]{2,1,0:T(8,128)(2,1)S(1)}, bf16[1,1024,128]{2,1,0:T(8,128)(2,1)S(1)}, u32[]{:S(2)}, u32[]{:S(2)}) collective-permute-start(bf16[1,1024,128]{2,1,0:T(8,128)(2,1)S(1)} %get-tuple-element.30), channel_id=1, source_target_pairs={{0,2},{1,3},{2,0},{3,1},{4,6},{5,7},{6,4},{7,5},{8,10},{9,11},{10,... | collective-permute-start | bytes 786440 | tf_op jit(solution)/shard_map/ppermute | solution.py:32
  106.9 18.7 %collective-permute-start.6 = (bf16[1,1024,128]{2,1,0:T(8,128)(2,1)S(1)}, bf16[1,1024,128]{2,1,0:T(8,128)(2,1)S(1)}, u32[]{:S(2)}, u32[]{:S(2)}) collective-permute-start(bf16[1,1024,128]{2,1,0:T(8,128)(2,1)S(1)} %get-tuple-element.29), channel_id=1, source_target_pairs={{0,3},{1,2},{2,1},{3,0},{4,7},{5,6},{6,5},{7,4},{8,11},{9,10},{10,... | collective-permute-start | bytes 786440 | tf_op jit(solution)/shard_map/ppermute | solution.py:32
